TPU v7x, 32 devices: a whole 2x2x4 slice. The times are simulated.
32 devices in a mesh: region: 2 (over y), tile: 4 (over z), shot: 2 (over x), pair: 2 (over core).
Axes of the slice: x: 2, y: 2, z: 4, core: 2. Of those that a mesh axis runs over, the one named last changes fastest.
Arguments:
- velocity: float32 [64, 128, 128], P(('region', 'tile'), ('shot', 'pair')), parts along dimension 0, may hold values from 1.5 to 4.5
- anchors: int32 [4], P(('region', 'shot')), parts along dimension 0, may hold values from 0 to 64, as said below
- source_prev: float32 [8, 32, 64, 128], P(('region', 'shot', 'pair'), 'tile'), parts along dimension 0, may hold values from -6 to 6
- source_now: float32 [8, 32, 64, 128], P(('region', 'shot', 'pair'), 'tile'), parts along dimension 0, may hold values from -6 to 6
- recv_prev: float32 [8, 32, 64, 128], P(('region', 'shot', 'pair'), 'tile'), parts along dimension 0, may hold values from -6 to 6
- recv_now: float32 [8, 32, 64, 128], P(('region', 'shot', 'pair'), 'tile'), parts along dimension 0, may hold values from -6 to 6
- source_x: int32 [8], P(('region', 'shot', 'pair')), parts along dimension 0, may hold values from 0 to 31
- source_yz: int32 [8], P(('region', 'shot', 'pair')), parts along dimension 0, may hold values from 0 to 8191
- wavelet: float32 [8, 6], P(('region', 'shot', 'pair')), parts along dimension 0, may hold values from -6 to 6
- recv_x: int32 [8, 128], P(('region', 'shot', 'pair')), parts along dimension 0, may hold values from 0 to 31
- recv_yz: int32 [8, 128], P(('region', 'shot', 'pair')), parts along dimension 0, may hold values from 0 to 8191
- record: float32 [8, 6, 128], P(('region', 'shot', 'pair')), parts along dimension 0, may hold values from -6 to 6
Outputs:
- image: float32 [64, 128, 128], P(('region', 'tile'), ('shot', 'pair')), parts along dimension 0
- source_field: float32 [8, 32, 64, 128], P(('region', 'shot', 'pair'), 'tile'), parts along dimension 0
- receiver_field: float32 [8, 32, 64, 128], P(('region', 'shot', 'pair'), 'tile'), parts along dimension 0
There are 2 independent parts, one for each index of `region`. A program takes and returns all parts, laid end to end along the dimension named above; each array names one. Nothing has to cross between parts.
Inputs may be any that keep to these rules, and one draw needn't show every extreme that they name: Aperture a covers survey rows anchors[a] to anchors[a] + 63 along the second dimension; in every draw some aperture starts at 64.
All inputs are finite; a program needn't handle non-finite values.
Results may differ from a plain program's by a relative error of at most 0.00002.
Values sent between devices are 32-bit elements; how exact they have to be, the bound alone decides.
A program may use at most 64 MiB of HBM per device.

v0:
```python
import jax
import jax.numpy as jnp
from jax import lax
from jax.sharding import PartitionSpec as P

STEPS = 6


stencil_weights = (-205.0 / 72.0, 8.0 / 5.0, -1.0 / 5.0, 8.0 / 315.0, -1.0 / 560.0)
courant_scale = 0.1


def padded_2(cells, sides, width):
    for axis, dim in sides:
        count = lax.axis_size(axis)
        ends = count - 1
        head = lax.slice_in_dim(cells, 0, width, axis=dim)
        tail = lax.slice_in_dim(cells, cells.shape[dim] - width, cells.shape[dim], axis=dim)
        cells = jnp.concatenate(
            [
                lax.ppermute(tail, axis, [(i, (i + 1) % count) for i in range(ends)]),
                cells,
                lax.ppermute(head, axis, [((i + 1) % count, i) for i in range(ends)]),
            ],
            axis=dim,
        )
    return cells


def laplace(extended):
    length = extended.shape[1]
    across = extended.shape[2]
    downward = extended.shape[3]
    interior = length - 8
    padded = jnp.pad(extended, ((0, 0), (0, 0), (4, 4), (4, 4)))

    def sample(along_x, along_y, along_z):
        return padded[
            :,
            4 + along_x : 4 + along_x + interior,
            4 + along_y : 4 + along_y + across,
            4 + along_z : 4 + along_z + downward,
        ]

    total = 3.0 * stencil_weights[0] * sample(0, 0, 0)
    for reach in range(1, 5):
        neighbour_sum = (
            sample(reach, 0, 0)
            + sample(-reach, 0, 0)
            + sample(0, reach, 0)
            + sample(0, -reach, 0)
            + sample(0, 0, reach)
            + sample(0, 0, -reach)
        )
        total = total + stencil_weights[reach] * neighbour_sum
    return total


def deposit(plane, columns, planes, amounts, leftmost):
    plane_cells = plane.shape[1] * plane.shape[2]
    local_column = columns - leftmost
    valid = (local_column >= 0) & (local_column < plane.shape[0])
    target = jnp.where(valid, local_column * plane_cells + planes, plane.shape[0] * plane_cells)
    return plane.reshape(-1).at[target].add(amounts, mode="drop").reshape(plane.shape)


def shards(
    velocity,
    anchors,
    source_prev,
    source_now,
    recv_prev,
    recv_now,
    source_x,
    source_yz,
    wavelet,
    recv_x,
    recv_yz,
    record,
):
    width = source_now.shape[1]
    across = source_now.shape[2]
    downward = source_now.shape[3]
    gathered = lax.all_gather(velocity, ("shot", "pair"), axis=1, tiled=True)
    start_row = anchors[0]
    window = lax.dynamic_slice_in_dim(gathered, start_row, across, 1)
    scaled = window * courant_scale
    courant = scaled * scaled
    first_column = lax.axis_index("tile") * width
    older = jnp.stack([source_prev[0], recv_prev[0]])
    current = jnp.stack([source_now[0], recv_now[0]])
    image = jnp.zeros((width, across, downward), jnp.float32)
    for moment in range(STEPS):
        extended = padded_2(current, (("tile", 1),), 4)
        interior = extended[:, 4 : extended.shape[1] - 4]
        updated = 2.0 * interior - older + courant * laplace(extended)
        source_part = deposit(updated[0], source_x, source_yz, wavelet[:, moment], first_column)
        receiver_part = deposit(updated[1], recv_x[0], recv_yz[0], record[0, moment], first_column)
        updated = jnp.stack([source_part, receiver_part])
        image = image + updated[0] * updated[1]
        older, current = (current, updated)
    canvas = jnp.zeros((width, gathered.shape[1], downward), jnp.float32)
    placed = lax.dynamic_update_slice_in_dim(canvas, image, start_row, 1)
    owned = lax.psum_scatter(placed, ("shot", "pair"), scatter_dimension=1, tiled=True)
    return (owned, current[0][None], current[1][None])


def solution(mesh):
    in_specs = (
        P(("region", "tile"), ("shot", "pair"), None),
        P(("region", "shot")),
        P(("region", "shot", "pair"), "tile", None, None),
        P(("region", "shot", "pair"), "tile", None, None),
        P(("region", "shot", "pair"), "tile", None, None),
        P(("region", "shot", "pair"), "tile", None, None),
        P(("region", "shot", "pair")),
        P(("region", "shot", "pair")),
        P(("region", "shot", "pair"), None),
        P(("region", "shot", "pair"), None),
        P(("region", "shot", "pair"), None),
        P(("region", "shot", "pair"), None, None),
    )
    out_specs = (
        P(("region", "tile"), ("shot", "pair"), None),
        P(("region", "shot", "pair"), "tile", None, None),
        P(("region", "shot", "pair"), "tile", None, None),
    )
    return jax.shard_map(shards, mesh=mesh, in_specs=in_specs, out_specs=out_specs, check_vma=False)
```

profile of v0, /device:TPU:0, one launch (start us, length us, event | category | flops | bytes accessed | tf_op | source)
XLA Modules:
  0.0 157.4 jit_solution(2351017794827974289)
XLA Ops:
  7.3 1.0 constant_dynamic-update-slice_fusion.1
  8.2 1.0 constant_dynamic-update-slice_fusion
  9.2 1.3 collective-permute-start
  10.5 6.3 %collective-permute-start.1 = (f32[2,4,64,128]{3,2,1,0:T(8,128)S(1)}, f32[2,4,64,128]{3,2,1,0:T(8,128)}, u32[]{:S(2)}, u32[]{:S(2)}) collective-permute-start(f32[2,4,64,128]{3,2,1,0:T(8,128)S(1)} %get-tuple-element.108), channel_id=1, source_target_pairs={{0,4},{4,8},{8,12},{1,5},{5,9},{9,13},{2,6},{6,10},{10,14},{3,7},{... | collective-permute-start | bytes 786440 | tf_op jit(solution)/shard_map/ppermute | solution.py:21
  17.5 7.8 %all_gather.3 = f32[8,128,128]{2,1,0:T(8,128)S(1)} all-gather(f32[8,32,128]{2,1,0:T(8,128)} %param.24), channel_id=1, replica_groups=mesh['region'=2,'tile'=4,'shot'=2,'pair'=2] {'shot','pair'}, dimensions={1}, use_global_device_ids=true | all-gather | bytes 655360 | tf_op jit(solution)/shard_map/all_gather | solution.py:84
  27.9 1.6 %select_maximum_fusion.15 = f32[2,16,72,136]{3,2,1,0:T(8,128)S(1)} fusion(f32[2,4,64,128]{3,2,1,0:T(8,128)S(1)} %collective-permute-done, f32[2,8,64,128]{3,2,1,0:T(8,128)S(1)} %constant_dynamic-update-slice_fusion, f32[2,4,64,128]{3,2,1,0:T(8,128)} %collective-permute-done.1), kind=kLoop, calls=%fused_computation.25 | loop fusion | flops 4700160 | bytes 2301952 | tf_op jit(solution)/shard_map/concatenate | solution.py:19
  29.5 4.1 %fusion.13 = f32[2,8,64,128]{3,2,1,0:T(8,128)} fusion(f32[2,8,64,128]{3,2,1,0:T(8,128)S(1)} %constant_dynamic-update-slice_fusion, f32[2,4,64,128]{3,2,1,0:T(8,128)} %collective-permute-done.1, f32[2,4,64,128]{3,2,1,0:T(8,128)S(1)} %collective-permute-done, f32[2,16,72,136]{3,2,1,0:T(8,128)S(1)} %select_maximum_fusion.15, f32[1,8,64,128]{3,2,1,0:T(8,128)} %param.28, ...), kind=kLoop, calls=%fused_computation.87 | loop fusion | flops 5505024 | bytes 10747904 | tf_op jit(solution)/shard_map/add | solution.py:96
  33.7 1.1 fusion.107
  34.7 2.1 %fusion.95 = f32[65536]{0:T(1024)S(1)} fusion(f32[65536]{0:T(1024)S(1)} %bitcast.106, s32[]{:T(128)} %bitcast.3, f32[1,1]{1,0:T(1,128)} %get-tuple-element.119, s32[1]{0:T(128)} %compare_select_fusion.1), kind=kLoop, calls=%fused_computation.291 | loop fusion | flops 5 | bytes 1036 | tf_op jit(solution)/shard_map/scatter-add | solution.py:64
  36.8 1.4 scatter_fusion
  38.3 1.3 collective-permute-start.2
  39.6 4.6 %collective-permute-start.3 = (f32[2,4,64,128]{3,2,1,0:T(8,128)S(1)}, f32[2,4,64,128]{3,2,1,0:T(8,128)S(1)}, u32[]{:S(2)}, u32[]{:S(2)}) collective-permute-start(f32[2,4,64,128]{3,2,1,0:T(8,128)S(1)} %get-tuple-element.103), channel_id=1, source_target_pairs={{0,4},{4,8},{8,12},{1,5},{5,9},{9,13},{2,6},{6,10},{10,14},{3,7},{... | collective-permute-start | bytes 786440 | tf_op jit(solution)/shard_map/ppermute | solution.py:21
  44.1 4.6 %collective-permute-done.2 = f32[2,4,64,128]{3,2,1,0:T(8,128)S(1)} collective-permute-done((f32[2,4,64,128]{3,2,1,0:T(8,128)S(1)}, f32[2,4,64,128]{3,2,1,0:T(8,128)S(1)}, u32[]{:S(2)}, u32[]{:S(2)}) %collective-permute-start.2) | collective-permute-done | bytes 262176 | tf_op jit(solution)/shard_map/ppermute | solution.py:23
  48.7 1.2 collective-permute-done.3
  50.8 2.1 %fusion.76 = f32[2,8,64,128]{3,2,1,0:T(8,128)S(1)} fusion(f32[2,16,72,136]{3,2,1,0:T(8,128)S(1)} %select_maximum_fusion.12, f32[2,12,64,128]{3,2,1,0:T(8,128)S(1)} %get-tuple-element.102, f32[2,12,64,128]{3,2,1,0:T(8,128)S(1)} %get-tuple-element.101, f32[2,8,64,128]{3,2,1,0:T(8,128)S(1)} %constant_dynamic-update-slice_fusion, ...), kind=kLoop, calls=%fused_computation.231 | loop fusion | flops 4456448 | bytes 14417920 | tf_op jit(solution)/shard_map/add | solution.py:96
  53.0 1.4 scatter_fusion.1
  54.4 2.1 %fusion.96 = f32[65536]{0:T(1024)S(1)} fusion(f32[65536]{0:T(1024)S(1)} %bitcast.88, s32[]{:T(128)} %bitcast.3, f32[1,1]{1,0:T(1,128)} %get-tuple-element.118, s32[1]{0:T(128)} %compare_select_fusion.1), kind=kLoop, calls=%fused_computation.292 | loop fusion | flops 5 | bytes 1036 | tf_op jit(solution)/shard_map/scatter-add | solution.py:64
  56.5 1.3 collective-permute-start.4
  57.8 5.0 %collective-permute-start.5 = (f32[2,4,64,128]{3,2,1,0:T(8,128)S(1)}, f32[2,4,64,128]{3,2,1,0:T(8,128)S(1)}, u32[]{:S(2)}, u32[]{:S(2)}) collective-permute-start(f32[2,4,64,128]{3,2,1,0:T(8,128)S(1)} %get-tuple-element.97), channel_id=1, source_target_pairs={{0,4},{4,8},{8,12},{1,5},{5,9},{9,13},{2,6},{6,10},{10,14},{3,7},{... | collective-permute-start | bytes 786440 | tf_op jit(solution)/shard_map/ppermute | solution.py:21
  62.8 3.7 %collective-permute-done.4 = f32[2,4,64,128]{3,2,1,0:T(8,128)S(1)} collective-permute-done((f32[2,4,64,128]{3,2,1,0:T(8,128)S(1)}, f32[2,4,64,128]{3,2,1,0:T(8,128)S(1)}, u32[]{:S(2)}, u32[]{:S(2)}) %collective-permute-start.4) | collective-permute-done | bytes 262176 | tf_op jit(solution)/shard_map/ppermute | solution.py:23
  66.6 1.2 collective-permute-done.5
  68.6 2.1 %fusion.66 = f32[2,8,64,128]{3,2,1,0:T(8,128)S(1)} fusion(f32[2,16,72,136]{3,2,1,0:T(8,128)S(1)} %select_maximum_fusion.9, f32[2,12,64,128]{3,2,1,0:T(8,128)S(1)} %get-tuple-element.96, f32[2,12,64,128]{3,2,1,0:T(8,128)S(1)} %get-tuple-element.95, f32[1,8,64,128]{3,2,1,0:T(8,128)S(1)} %bitcast.69, f32[1,8,64,128]{3,2,1,0:T(8,128)S(1)} %bitcast.92, ...), kind=kLoop, calls=%fused_computation.201 | loop fusion | flops 4587520 | bytes 14417920 | tf_op jit(solution)/shard_map/add | solution.py:96
  70.8 1.4 scatter_fusion.2
  72.1 2.2 %fusion.97 = f32[65536]{0:T(1024)S(1)} fusion(f32[65536]{0:T(1024)S(1)} %bitcast.94, s32[]{:T(128)} %bitcast.3, f32[1,1]{1,0:T(1,128)} %get-tuple-element.117, s32[1]{0:T(128)} %compare_select_fusion.1), kind=kLoop, calls=%fused_computation.293 | loop fusion | flops 5 | bytes 1036 | tf_op jit(solution)/shard_map/scatter-add | solution.py:64
  74.4 1.3 collective-permute-start.6
  75.7 5.0 %collective-permute-start.7 = (f32[2,4,64,128]{3,2,1,0:T(8,128)S(1)}, f32[2,4,64,128]{3,2,1,0:T(8,128)S(1)}, u32[]{:S(2)}, u32[]{:S(2)}) collective-permute-start(f32[2,4,64,128]{3,2,1,0:T(8,128)S(1)} %get-tuple-element.91), channel_id=1, source_target_pairs={{0,4},{4,8},{8,12},{1,5},{5,9},{9,13},{2,6},{6,10},{10,14},{3,7},{... | collective-permute-start | bytes 786440 | tf_op jit(solution)/shard_map/ppermute | solution.py:21
  80.8 2.8 %collective-permute-done.6 = f32[2,4,64,128]{3,2,1,0:T(8,128)S(1)} collective-permute-done((f32[2,4,64,128]{3,2,1,0:T(8,128)S(1)}, f32[2,4,64,128]{3,2,1,0:T(8,128)S(1)}, u32[]{:S(2)}, u32[]{:S(2)}) %collective-permute-start.6) | collective-permute-done | bytes 262176 | tf_op jit(solution)/shard_map/ppermute | solution.py:23
  83.6 1.2 collective-permute-done.7
  84.9 0.7 select_maximum_fusion.6
  85.6 2.1 %fusion.56 = f32[2,8,64,128]{3,2,1,0:T(8,128)S(1)} fusion(f32[2,16,72,136]{3,2,1,0:T(8,128)S(1)} %select_maximum_fusion.6, f32[2,12,64,128]{3,2,1,0:T(8,128)S(1)} %get-tuple-element.90, f32[2,12,64,128]{3,2,1,0:T(8,128)S(1)} %get-tuple-element.89, f32[1,8,64,128]{3,2,1,0:T(8,128)S(1)} %bitcast.75, f32[1,8,64,128]{3,2,1,0:T(8,128)S(1)} %bitcast.98, ...), kind=kLoop, calls=%fused_computation.171 | loop fusion | flops 4587520 | bytes 14417920 | tf_op jit(solution)/shard_map/add | solution.py:96
  87.8 1.4 scatter_fusion.3
  89.2 2.1 %fusion.98 = f32[65536]{0:T(1024)S(1)} fusion(f32[65536]{0:T(1024)S(1)} %bitcast.100, s32[]{:T(128)} %bitcast.3, f32[1,1]{1,0:T(1,128)} %get-tuple-element.116, s32[1]{0:T(128)} %compare_select_fusion.1), kind=kLoop, calls=%fused_computation.294 | loop fusion | flops 5 | bytes 1036 | tf_op jit(solution)/shard_map/scatter-add | solution.py:64
  91.4 1.3 collective-permute-start.8
  92.7 5.0 %collective-permute-start.9 = (f32[2,4,64,128]{3,2,1,0:T(8,128)S(1)}, f32[2,4,64,128]{3,2,1,0:T(8,128)S(1)}, u32[]{:S(2)}, u32[]{:S(2)}) collective-permute-start(f32[2,4,64,128]{3,2,1,0:T(8,128)S(1)} %get-tuple-element.85), channel_id=1, source_target_pairs={{0,4},{4,8},{8,12},{1,5},{5,9},{9,13},{2,6},{6,10},{10,14},{3,7},{... | collective-permute-start | bytes 786440 | tf_op jit(solution)/shard_map/ppermute | solution.py:21
  97.7 2.4 %collective-permute-done.8 = f32[2,4,64,128]{3,2,1,0:T(8,128)S(1)} collective-permute-done((f32[2,4,64,128]{3,2,1,0:T(8,128)S(1)}, f32[2,4,64,128]{3,2,1,0:T(8,128)S(1)}, u32[]{:S(2)}, u32[]{:S(2)}) %collective-permute-start.8) | collective-permute-done | bytes 262176 | tf_op jit(solution)/shard_map/ppermute | solution.py:23
  100.1 1.5 collective-permute-done.9
  102.4 2.1 %fusion.46 = f32[2,8,64,128]{3,2,1,0:T(8,128)S(1)} fusion(f32[2,16,72,136]{3,2,1,0:T(8,128)S(1)} %select_maximum_fusion.3, f32[2,12,64,128]{3,2,1,0:T(8,128)S(1)} %get-tuple-element.84, f32[2,12,64,128]{3,2,1,0:T(8,128)S(1)} %get-tuple-element.83, f32[1,8,64,128]{3,2,1,0:T(8,128)S(1)} %bitcast.81, f32[1,8,64,128]{3,2,1,0:T(8,128)S(1)} %bitcast.104, ...), kind=kLoop, calls=%fused_computation.141 | loop fusion | flops 4587520 | bytes 14417920 | tf_op jit(solution)/shard_map/add | solution.py:96
  104.6 1.4 scatter_fusion.4
  106.0 2.1 %fusion.99 = f32[65536]{0:T(1024)S(1)} fusion(f32[65536]{0:T(1024)S(1)} %bitcast.112, s32[]{:T(128)} %bitcast.3, f32[1,1]{1,0:T(1,128)} %get-tuple-element.120, s32[1]{0:T(128)} %compare_select_fusion.1), kind=kLoop, calls=%fused_computation.295 | loop fusion | flops 5 | bytes 1036 | tf_op jit(solution)/shard_map/scatter-add | solution.py:64
  108.1 1.3 collective-permute-start.10
  109.4 5.0 %collective-permute-start.11 = (f32[2,4,64,128]{3,2,1,0:T(8,128)S(1)}, f32[2,4,64,128]{3,2,1,0:T(8,128)S(1)}, u32[]{:S(2)}, u32[]{:S(2)}) collective-permute-start(f32[2,4,64,128]{3,2,1,0:T(8,128)S(1)} %get-tuple-element.79), channel_id=1, source_target_pairs={{0,4},{4,8},{8,12},{1,5},{5,9},{9,13},{2,6},{6,10},{10,14},{3,7},{... | collective-permute-start | bytes 786440 | tf_op jit(solution)/shard_map/ppermute | solution.py:21
  114.4 2.4 %collective-permute-done.10 = f32[2,4,64,128]{3,2,1,0:T(8,128)S(1)} collective-permute-done((f32[2,4,64,128]{3,2,1,0:T(8,128)S(1)}, f32[2,4,64,128]{3,2,1,0:T(8,128)S(1)}, u32[]{:S(2)}, u32[]{:S(2)}) %collective-permute-start.10) | collective-permute-done | bytes 262176 | tf_op jit(solution)/shard_map/ppermute | solution.py:23
  116.8 1.5 collective-permute-done.11
  119.2 2.1 %fusion.36 = f32[2,8,64,128]{3,2,1,0:T(8,128)S(1)} fusion(f32[2,16,72,136]{3,2,1,0:T(8,128)S(1)} %select_maximum_fusion, f32[2,12,64,128]{3,2,1,0:T(8,128)S(1)} %get-tuple-element.78, f32[2,12,64,128]{3,2,1,0:T(8,128)S(1)} %get-tuple-element.77, f32[1,8,64,128]{3,2,1,0:T(8,128)S(1)} %bitcast.87, f32[1,8,64,128]{3,2,1,0:T(8,128)S(1)} %bitcast.116, ...), kind=kLoop, calls=%fused_computation.111 | loop fusion | flops 4587520 | bytes 14417920 | tf_op jit(solution)/shard_map/add | solution.py:96
  121.4 1.4 scatter_fusion.5
  122.8 2.2 %fusion.100 = f32[65536]{0:T(1024)S(1)} fusion(f32[65536]{0:T(1024)S(1)} %bitcast.119, s32[]{:T(128)} %bitcast.3, f32[1,1]{1,0:T(1,128)} %get-tuple-element.115, s32[1]{0:T(128)} %compare_select_fusion.1), kind=kLoop, calls=%fused_computation.296 | loop fusion | flops 5 | bytes 1036 | tf_op jit(solution)/shard_map/scatter-add | solution.py:64
  125.6 0.8 copy-done.1
  126.4 24.2 %reduce-scatter.2.cloned.1.call-done = f32[8,32,128]{2,1,0:T(8,128)} async-done(((f32[8,128,128]{2,1,0:T(8,128)}), f32[8,32,128]{2,1,0:T(8,128)}) %reduce-scatter.2.cloned.1.call-update) | async-done | bytes 131088 | tf_op jit(solution)/shard_map/reduce_scatter | solution.py:104
  (44 shorter events, 5.5 us)
Async XLA Ops:
  7.2 18.2 %copy-start.6 = (s32[1,128]{1,0:T(1,128)S(1)}, s32[1,128]{1,0:T(1,128)}, u32[]{:S(2)}) copy-start(s32[1,128]{1,0:T(1,128)} %param.33) | copy-start | bytes 1540
  7.2 18.2 %copy-start.5 = (s32[1,128]{1,0:T(1,128)S(1)}, s32[1,128]{1,0:T(1,128)}, u32[]{:S(2)}) copy-start(s32[1,128]{1,0:T(1,128)} %param.34) | copy-start | bytes 1540
  7.2 18.2 %copy-start.3 = (f32[1,6]{1,0:T(1,128)S(1)}, f32[1,6]{1,0:T(1,128)}, u32[]{:S(2)}) copy-start(f32[1,6]{1,0:T(1,128)} %param.32) | copy-start | bytes 76
  7.2 20.7 %copy-start.4 = (f32[1,6,128]{2,0,1:T(1,128)S(1)}, f32[1,6,128]{2,0,1:T(1,128)}, u32[]{:S(2)}) copy-start(f32[1,6,128]{2,0,1:T(1,128)} %param.35) | copy-start | bytes 9220
  7.2 143.3 %reduce-scatter.2.cloned.1.call-start = ((), (), s32[]{:S(2)}) async-start(), calls=%async_computation.1 | async-start | bytes 655360 | tf_op jit(solution)/shard_map/reduce_scatter | solution.py:104
  9.2 18.6 %collective-permute-start = (f32[2,4,64,128]{3,2,1,0:T(8,128)S(1)}, f32[2,4,64,128]{3,2,1,0:T(8,128)S(1)}, u32[]{:S(2)}, u32[]{:S(2)}) collective-permute-start(f32[2,4,64,128]{3,2,1,0:T(8,128)S(1)} %get-tuple-element.107), channel_id=1, source_target_pairs={{4,0},{8,4},{12,8},{5,1},{9,5},{13,9},{6,2},{10,6},{14,10},{7,3},{... | collective-permute-start | bytes 786440 | tf_op jit(solution)/shard_map/ppermute | solution.py:23
  10.5 17.3 %collective-permute-start.1 = (f32[2,4,64,128]{3,2,1,0:T(8,128)S(1)}, f32[2,4,64,128]{3,2,1,0:T(8,128)}, u32[]{:S(2)}, u32[]{:S(2)}) collective-permute-start(f32[2,4,64,128]{3,2,1,0:T(8,128)S(1)} %get-tuple-element.108), channel_id=1, source_target_pairs={{0,4},{4,8},{8,12},{1,5},{5,9},{9,13},{2,6},{6,10},{10,14},{3,7},{... | collective-permute-start | bytes 786440 | tf_op jit(solution)/shard_map/ppermute | solution.py:21
  38.3 10.4 %collective-permute-start.2 = (f32[2,4,64,128]{3,2,1,0:T(8,128)S(1)}, f32[2,4,64,128]{3,2,1,0:T(8,128)S(1)}, u32[]{:S(2)}, u32[]{:S(2)}) collective-permute-start(f32[2,4,64,128]{3,2,1,0:T(8,128)S(1)} %get-tuple-element.104), channel_id=1, source_target_pairs={{4,0},{8,4},{12,8},{5,1},{9,5},{13,9},{6,2},{10,6},{14,10},{7,3},{... | collective-permute-start | bytes 786440 | tf_op jit(solution)/shard_map/ppermute | solution.py:23
  39.6 10.3 %collective-permute-start.3 = (f32[2,4,64,128]{3,2,1,0:T(8,128)S(1)}, f32[2,4,64,128]{3,2,1,0:T(8,128)S(1)}, u32[]{:S(2)}, u32[]{:S(2)}) collective-permute-start(f32[2,4,64,128]{3,2,1,0:T(8,128)S(1)} %get-tuple-element.103), channel_id=1, source_target_pairs={{0,4},{4,8},{8,12},{1,5},{5,9},{9,13},{2,6},{6,10},{10,14},{3,7},{... | collective-permute-start | bytes 786440 | tf_op jit(solution)/shard_map/ppermute | solution.py:21
  56.5 10.1 %collective-permute-start.4 = (f32[2,4,64,128]{3,2,1,0:T(8,128)S(1)}, f32[2,4,64,128]{3,2,1,0:T(8,128)S(1)}, u32[]{:S(2)}, u32[]{:S(2)}) collective-permute-start(f32[2,4,64,128]{3,2,1,0:T(8,128)S(1)} %get-tuple-element.98), channel_id=1, source_target_pairs={{4,0},{8,4},{12,8},{5,1},{9,5},{13,9},{6,2},{10,6},{14,10},{7,3},{... | collective-permute-start | bytes 786440 | tf_op jit(solution)/shard_map/ppermute | solution.py:23
  57.8 9.9 %collective-permute-start.5 = (f32[2,4,64,128]{3,2,1,0:T(8,128)S(1)}, f32[2,4,64,128]{3,2,1,0:T(8,128)S(1)}, u32[]{:S(2)}, u32[]{:S(2)}) collective-permute-start(f32[2,4,64,128]{3,2,1,0:T(8,128)S(1)} %get-tuple-element.97), channel_id=1, source_target_pairs={{0,4},{4,8},{8,12},{1,5},{5,9},{9,13},{2,6},{6,10},{10,14},{3,7},{... | collective-permute-start | bytes 786440 | tf_op jit(solution)/shard_map/ppermute | solution.py:21
  74.4 9.1 %collective-permute-start.6 = (f32[2,4,64,128]{3,2,1,0:T(8,128)S(1)}, f32[2,4,64,128]{3,2,1,0:T(8,128)S(1)}, u32[]{:S(2)}, u32[]{:S(2)}) collective-permute-start(f32[2,4,64,128]{3,2,1,0:T(8,128)S(1)} %get-tuple-element.92), channel_id=1, source_target_pairs={{4,0},{8,4},{12,8},{5,1},{9,5},{13,9},{6,2},{10,6},{14,10},{7,3},{... | collective-permute-start | bytes 786440 | tf_op jit(solution)/shard_map/ppermute | solution.py:23
  75.7 9.0 %collective-permute-start.7 = (f32[2,4,64,128]{3,2,1,0:T(8,128)S(1)}, f32[2,4,64,128]{3,2,1,0:T(8,128)S(1)}, u32[]{:S(2)}, u32[]{:S(2)}) collective-permute-start(f32[2,4,64,128]{3,2,1,0:T(8,128)S(1)} %get-tuple-element.91), channel_id=1, source_target_pairs={{0,4},{4,8},{8,12},{1,5},{5,9},{9,13},{2,6},{6,10},{10,14},{3,7},{... | collective-permute-start | bytes 786440 | tf_op jit(solution)/shard_map/ppermute | solution.py:21
  91.4 8.7 %collective-permute-start.8 = (f32[2,4,64,128]{3,2,1,0:T(8,128)S(1)}, f32[2,4,64,128]{3,2,1,0:T(8,128)S(1)}, u32[]{:S(2)}, u32[]{:S(2)}) collective-permute-start(f32[2,4,64,128]{3,2,1,0:T(8,128)S(1)} %get-tuple-element.86), channel_id=1, source_target_pairs={{4,0},{8,4},{12,8},{5,1},{9,5},{13,9},{6,2},{10,6},{14,10},{7,3},{... | collective-permute-start | bytes 786440 | tf_op jit(solution)/shard_map/ppermute | solution.py:23
  92.7 8.9 %collective-permute-start.9 = (f32[2,4,64,128]{3,2,1,0:T(8,128)S(1)}, f32[2,4,64,128]{3,2,1,0:T(8,128)S(1)}, u32[]{:S(2)}, u32[]{:S(2)}) collective-permute-start(f32[2,4,64,128]{3,2,1,0:T(8,128)S(1)} %get-tuple-element.85), channel_id=1, source_target_pairs={{0,4},{4,8},{8,12},{1,5},{5,9},{9,13},{2,6},{6,10},{10,14},{3,7},{... | collective-permute-start | bytes 786440 | tf_op jit(solution)/shard_map/ppermute | solution.py:21
  108.1 8.7 %collective-permute-start.10 = (f32[2,4,64,128]{3,2,1,0:T(8,128)S(1)}, f32[2,4,64,128]{3,2,1,0:T(8,128)S(1)}, u32[]{:S(2)}, u32[]{:S(2)}) collective-permute-start(f32[2,4,64,128]{3,2,1,0:T(8,128)S(1)} %get-tuple-element.80), channel_id=1, source_target_pairs={{4,0},{8,4},{12,8},{5,1},{9,5},{13,9},{6,2},{10,6},{14,10},{7,3},{... | collective-permute-start | bytes 786440 | tf_op jit(solution)/shard_map/ppermute | solution.py:23
  109.4 8.9 %collective-permute-start.11 = (f32[2,4,64,128]{3,2,1,0:T(8,128)S(1)}, f32[2,4,64,128]{3,2,1,0:T(8,128)S(1)}, u32[]{:S(2)}, u32[]{:S(2)}) collective-permute-start(f32[2,4,64,128]{3,2,1,0:T(8,128)S(1)} %get-tuple-element.79), channel_id=1, source_target_pairs={{0,4},{4,8},{8,12},{1,5},{5,9},{9,13},{2,6},{6,10},{10,14},{3,7},{... | collective-permute-start | bytes 786440 | tf_op jit(solution)/shard_map/ppermute | solution.py:21
  122.7 3.6 %copy-start = (f32[65536]{0:T(1024)}, f32[65536]{0:T(1024)S(1)}, u32[]{:S(2)}) copy-start(f32[65536]{0:T(1024)S(1)} %scatter_fusion.5) | copy-start | bytes 786436
  124.9 1.5 copy-start.2
  125.6 0.8 copy-start.1
Sparse Core Ops, SparseCore 0:
  126.5 24.0 reduce-scatter.1
where the time goes:
time: 158 us; the launch traced here: 157 us
  waiting for transfers between devices  46.5 us (29%)
  other arithmetic  42.2 us (27%)
  starting transfers between devices  38.7 us (24%)
  between operations  17 us (11%)
  blocking collectives  7.82 us (5%)
  local copies, waits for them, and re-layouts  5.19 us (3%)
    ppermute x6, starting transfers between devices, padded_2(): lax.ppermute(tail, axis, [(i, (i + 1) % count) for i in range(ends)])  30.9 us
    reduce_scatter x1, waiting for transfers between devices, shards(): lax.psum_scatter(placed, ('shot', 'pair'), scatter_dimension=1, tiled=True)  24.2 us
    scatter-add x12, other arithmetic, deposit(): plane.reshape(-1).at[target].add(amounts, mode='drop').reshape(plane.shape)  21.1 us
    ppermute x6, waiting for transfers between devices, padded_2(): lax.ppermute(head, axis, [((i + 1) % count, i) for i in range(ends)])  15.9 us
    add x6, other arithmetic, shards(): updated = 2.0 * interior - older + courant * laplace(extended)  14.7 us
    all_gather x1, blocking collectives, shards(): gathered = lax.all_gather(velocity, ('shot', 'pair'), axis=1, tiled=True)  7.82 us
    ppermute x6, starting transfers between devices, padded_2(): lax.ppermute(head, axis, [((i + 1) % count, i) for i in range(ends)])  7.75 us
    ppermute x6, waiting for transfers between devices, padded_2(): lax.ppermute(tail, axis, [(i, (i + 1) % count) for i in range(ends)])  6.47 us
  transfers between devices with their start and end apart: 13, of which 11 were waited for; matrix products, arithmetic and copies ran while one was open for 0% of the time, Pallas kernels for 0%

commit v1 on v0

v1 whole, which is shorter than its diff:
```python
import functools

import jax
import jax.numpy as jnp
from jax import lax
from jax.experimental import pallas as pl
from jax.experimental.pallas import tpu as pltpu
from jax.sharding import PartitionSpec as P

STEPS = 6
MESH = pl.DeviceIdType.MESH

stencil_weights = (-205.0 / 72.0, 8.0 / 5.0, -1.0 / 5.0, 8.0 / 315.0, -1.0 / 560.0)
courant_scale = 0.1

PAD = 8
CHUNKS = 4


def kernel(
    sizes,
    anchors,
    source_x,
    source_yz,
    wavelet,
    recv_x,
    recv_yz,
    record,
    velocity,
    source_prev,
    source_now,
    recv_prev,
    recv_now,
    image_out,
    source_out,
    recv_out,
    field,
    speed,
    courant,
    injected,
    stacked,
    mate_out,
    mate_in,
    shot_out,
    shot_in,
    total,
    load_sem,
    halo_send,
    halo_recv,
    speed_send,
    speed_recv,
    mate_speed_send,
    mate_speed_recv,
    mate_sem,
    shot_send,
    shot_recv,
    out_sem,
):
    n_tile, n_shot, n_pair = sizes
    width, across, downward = source_now.shape[1:]
    owned = velocity.shape[1]
    survey = owned * n_shot * n_pair
    margin = survey - across
    rows = across // CHUNKS
    tile = lax.axis_index("tile")
    shot = lax.axis_index("shot")
    pair = lax.axis_index("pair")
    mate = 1 - pair
    has_low = tile > 0
    has_high = tile < n_tile - 1

    barrier = pltpu.get_barrier_semaphore()

    @pl.when(has_low)
    def _():
        pl.semaphore_signal(barrier, inc=1, device_id={"tile": tile - 1}, device_id_type=MESH)

    @pl.when(has_high)
    def _():
        pl.semaphore_signal(barrier, inc=1, device_id={"tile": tile + 1}, device_id_type=MESH)

    pl.semaphore_signal(barrier, inc=1, device_id={"pair": mate}, device_id_type=MESH)
    for k in range(1, n_shot):
        pl.semaphore_signal(barrier, inc=1, device_id={"shot": lax.rem(shot + k, n_shot)}, device_id_type=MESH)

    def owner_rows(s, p):
        return pl.ds(pl.multiple_of((s * n_pair + p) * owned, owned), owned)

    inner = pl.ds(PAD, across)
    loads = [
        pltpu.make_async_copy(source_now.at[0], field.at[0, 0, 4 : 4 + width, inner], load_sem.at[0]),
        pltpu.make_async_copy(recv_now.at[0], field.at[0, 1, 4 : 4 + width, inner], load_sem.at[1]),
        pltpu.make_async_copy(source_prev.at[0], field.at[1, 0, 4 : 4 + width, inner], load_sem.at[2]),
        pltpu.make_async_copy(recv_prev.at[0], field.at[1, 1, 4 : 4 + width, inner], load_sem.at[3]),
        pltpu.make_async_copy(velocity, speed.at[:, owner_rows(shot, pair)], load_sem.at[4]),
    ]
    for copy in loads:
        copy.start()

    neighbours = n_shot + has_low.astype(jnp.int32) + has_high.astype(jnp.int32)
    pl.semaphore_wait(barrier, neighbours)

    def start_halo(c, f, now):
        part = pl.ds(pl.multiple_of(c * rows, rows), rows)
        landing = pl.ds(pl.multiple_of(PAD + c * rows, 8), rows)

        @pl.when(has_low)
        def _():
            pltpu.make_async_remote_copy(
                now.at[0, 0:4, part],
                field.at[0, f, 4 + width : 8 + width, landing],
                halo_send.at[0, c, 0],
                halo_recv.at[0, c, 1],
                device_id={"tile": tile - 1},
                device_id_type=MESH,
            ).start()

        @pl.when(has_high)
        def _():
            pltpu.make_async_remote_copy(
                now.at[0, width - 4 : width, part],
                field.at[0, f, 0:4, landing],
                halo_send.at[0, c, 1],
                halo_recv.at[0, c, 0],
                device_id={"tile": tile + 1},
                device_id_type=MESH,
            ).start()

    def halo(n, slot, c, side):
        landing = pl.ds(pl.multiple_of(PAD + c * rows, 8), rows)
        if side == 0:
            source, target, other = pl.ds(4, 4), pl.ds(4 + width, 4), tile - 1
        else:
            source, target, other = pl.ds(width, 4), pl.ds(0, 4), tile + 1
        return pltpu.make_async_remote_copy(
            field.at[slot, :, source, landing],
            field.at[slot, :, target, landing],
            halo_send.at[n, c, side],
            halo_recv.at[n, c, 1 - side],
            device_id={"tile": other},
            device_id_type=MESH,
        )

    for k in range(1, n_shot):
        pltpu.make_async_remote_copy(
            velocity,
            speed.at[:, owner_rows(shot, pair)],
            speed_send.at[k],
            speed_recv.at[k],
            device_id={"shot": lax.rem(shot + k, n_shot)},
            device_id_type=MESH,
        ).start()
    pltpu.make_async_remote_copy(
        velocity,
        speed.at[:, owner_rows(shot, pair)],
        mate_speed_send.at[0],
        mate_speed_recv.at[0],
        device_id={"pair": mate},
        device_id_type=MESH,
    ).start()
    for c in range(CHUNKS):
        start_halo(c, 0, source_now)
        start_halo(c, 1, recv_now)

    for slot in range(2):
        for f in range(2):
            field[slot, f, 4 : 4 + width, 0:PAD] = jnp.zeros((width, PAD, downward), jnp.float32)
            field[slot, f, 4 : 4 + width, PAD + across : 2 * PAD + across] = jnp.zeros((width, PAD, downward), jnp.float32)

    def clear(first):
        def body(i, _):
            field[i // 8, (i // 4) % 2, first + i % 4] = jnp.zeros((across + 2 * PAD, downward), jnp.float32)
            return 0

        lax.fori_loop(0, 16, body, 0)

    @pl.when(jnp.logical_not(has_low))
    def _():
        clear(0)

    @pl.when(jnp.logical_not(has_high))
    def _():
        clear(4 + width)

    def clear_image(i, _):
        stacked[i] = jnp.zeros((2 * margin + across, downward), jnp.float32)
        return 0

    lax.fori_loop(0, width, clear_image, 0)

    first = tile * width
    place = (recv_x[...] - first) * across + recv_yz[...] // downward
    depth = recv_yz[...] % downward
    receivers = record.shape[2]
    cell = lax.broadcasted_iota(jnp.int32, (width * across, receivers), 0)
    pick = jnp.where(cell == place, 1.0, 0.0).astype(jnp.bfloat16)
    at_depth = lax.broadcasted_iota(jnp.int32, (downward, receivers), 0) == depth

    def inject(n, _):
        amount = record[0, pl.ds(n, 1), :]
        high = amount.astype(jnp.bfloat16).astype(jnp.float32)
        rest = amount - high
        middle = rest.astype(jnp.bfloat16).astype(jnp.float32)
        low = rest - middle
        dense = jnp.zeros((width * across, downward), jnp.float32)
        for piece in (low, middle, high):
            spread = jnp.where(at_depth, piece, 0.0).astype(jnp.bfloat16)
            dense = dense + lax.dot_general(
                pick, spread, (((1,), (1,)), ((), ())), preferred_element_type=jnp.float32
            )
        injected[n] = dense.reshape(width, across, downward)
        return 0

    lax.fori_loop(0, STEPS, inject, 0)

    for k in range(1, n_shot):
        origin = lax.rem(shot + n_shot - k, n_shot)
        block = speed.at[:, owner_rows(origin, pair)]
        pltpu.make_async_remote_copy(
            velocity, block, speed_send.at[k], speed_recv.at[k], device_id={"pair": mate}, device_id_type=MESH
        ).wait()
        pltpu.make_async_remote_copy(
            block, block, mate_speed_send.at[k], mate_speed_recv.at[k], device_id={"pair": mate}, device_id_type=MESH
        ).start()
    for copy in loads:
        copy.wait()
    for k in range(n_shot):
        origin = lax.rem(shot + n_shot - k, n_shot)
        pltpu.make_async_remote_copy(
            velocity,
            speed.at[:, owner_rows(origin, mate)],
            mate_speed_send.at[k],
            mate_speed_recv.at[k],
            device_id={"pair": mate},
            device_id_type=MESH,
        ).wait()

    start_row = anchors[0]

    def refresh(i, _):
        scaled = speed[i, pl.ds(start_row, across), :] * courant_scale
        courant[i] = scaled * scaled
        return 0

    lax.fori_loop(0, width, refresh, 0)

    lane = lax.broadcasted_iota(jnp.int32, (1, 1, downward), 2)
    behind = [jnp.where(lane >= r, stencil_weights[r], 0.0) for r in range(1, 5)]
    ahead = [jnp.where(lane < downward - r, stencil_weights[r], 0.0) for r in range(1, 5)]
    shape = (width, 8, downward)
    local_cell = (
        lax.broadcasted_iota(jnp.int32, shape, 0) * (across * downward)
        + lax.broadcasted_iota(jnp.int32, shape, 1) * downward
        + lax.broadcasted_iota(jnp.int32, shape, 2)
    )
    source_cell = (source_x[0] - first) * (across * downward) + source_yz[0]

    def update(s, slot, y0):
        at = pl.multiple_of(PAD + y0, 8)
        gain = courant[:, pl.ds(y0, 8), :]
        results = []
        for f in range(2):
            column = field[slot, f, :, pl.ds(at, 8), :]
            centre = column[4 : 4 + width]
            sums = (3.0 * stencil_weights[0]) * centre
            for r in range(1, 5):
                near = column[4 - r : 4 - r + width] + column[4 + r : 4 + r + width]
                near = near + field[slot, f, 4 : 4 + width, pl.ds(at - r, 8), :]
                near = near + field[slot, f, 4 : 4 + width, pl.ds(at + r, 8), :]
                sums = sums + stencil_weights[r] * near
                sums = sums + behind[r - 1] * pltpu.roll(centre, r, 2)
                sums = sums + ahead[r - 1] * pltpu.roll(centre, downward - r, 2)
            older = field[1 - slot, f, 4 : 4 + width, pl.ds(at, 8), :]
            fresh = 2.0 * centre - older + gain * sums
            if f == 0:
                fresh = fresh + jnp.where(local_cell == source_cell - y0 * downward, wavelet[0, s], 0.0)
            else:
                fresh = fresh + injected[s, :, pl.ds(y0, 8), :]
            field[1 - slot, f, 4 : 4 + width, pl.ds(at, 8), :] = fresh
            results.append(fresh)
        spot = pl.ds(pl.multiple_of(margin + y0, 8), 8)
        stacked[:, spot, :] = stacked[:, spot, :] + results[0] * results[1]

    def step(s, _):
        slot = lax.rem(s, 2)

        def chunk(c, _):
            @pl.when(has_low)
            def _():
                halo(s, slot, c, 1).wait_recv()

            @pl.when(has_high)
            def _():
                halo(s, slot, c, 0).wait_recv()

            @pl.when(jnp.logical_and(has_low, s > 0))
            def _():
                halo(s - 1, 1 - slot, c, 0).wait_send()

            @pl.when(jnp.logical_and(has_high, s > 0))
            def _():
                halo(s - 1, 1 - slot, c, 1).wait_send()

            def tiles(t, _):
                update(s, slot, pl.multiple_of(c * rows + t * 8, 8))
                return 0

            lax.fori_loop(0, rows // 8, tiles, 0)

            @pl.when(jnp.logical_and(has_low, s < STEPS - 1))
            def _():
                halo(s + 1, 1 - slot, c, 0).start()

            @pl.when(jnp.logical_and(has_high, s < STEPS - 1))
            def _():
                halo(s + 1, 1 - slot, c, 1).start()

            return 0

        lax.fori_loop(0, CHUNKS, chunk, 0)
        return 0

    lax.fori_loop(0, STEPS, step, 0)

    final = STEPS % 2
    stores = [
        pltpu.make_async_copy(field.at[final, 0, 4 : 4 + width, inner], source_out.at[0], out_sem.at[0]),
        pltpu.make_async_copy(field.at[final, 1, 4 : 4 + width, inner], recv_out.at[0], out_sem.at[1]),
    ]
    for copy in stores:
        copy.start()

    def contribution(s, p):
        return stacked[:, pl.ds((s * n_pair + p) * owned + margin - start_row, owned), :]

    for k in range(n_shot):
        mate_out[k] = contribution(lax.rem(shot + k, n_shot), mate)
        pltpu.make_async_remote_copy(
            mate_out.at[k],
            mate_in.at[k],
            mate_sem.at[0, k],
            mate_sem.at[1, k],
            device_id={"pair": mate},
            device_id_type=MESH,
        ).start()

    def mate_copy(k):
        return pltpu.make_async_remote_copy(
            mate_out.at[k],
            mate_in.at[k],
            mate_sem.at[0, k],
            mate_sem.at[1, k],
            device_id={"pair": mate},
            device_id_type=MESH,
        )

    def shot_copy(k):
        return pltpu.make_async_remote_copy(
            shot_out.at[k - 1],
            shot_in.at[k - 1],
            shot_send.at[k - 1],
            shot_recv.at[k - 1],
            device_id={"shot": lax.rem(shot + k, n_shot)},
            device_id_type=MESH,
        )

    for k in range(1, n_shot):
        mate_copy(k).wait_recv()
        shot_out[k - 1] = contribution(lax.rem(shot + k, n_shot), pair) + mate_in[k]
        shot_copy(k).start()
    mate_copy(0).wait_recv()
    mine = contribution(shot, pair) + mate_in[0]
    for k in range(1, n_shot):
        shot_copy(k).wait_recv()
        mine = mine + shot_in[k - 1]
    total[...] = mine
    last = pltpu.make_async_copy(total, image_out, out_sem.at[2])
    last.start()

    for c in range(CHUNKS):
        @pl.when(has_low)
        def _():
            halo(STEPS - 1, (STEPS - 1) % 2, c, 0).wait_send()

        @pl.when(has_high)
        def _():
            halo(STEPS - 1, (STEPS - 1) % 2, c, 1).wait_send()

    for k in range(n_shot):
        mate_copy(k).wait_send()
    for k in range(1, n_shot):
        shot_copy(k).wait_send()
    for copy in stores:
        copy.wait()
    last.wait()


def solution(mesh):
    sizes = (mesh.shape["tile"], mesh.shape["shot"], mesh.shape["pair"])
    n_shot, n_pair = sizes[1:]

    def shards(velocity, anchors, source_prev, source_now, recv_prev, recv_now, source_x, source_yz, wavelet, recv_x, recv_yz, record):
        width, across, downward = source_now.shape[1:]
        owned = velocity.shape[1]
        survey = owned * n_shot * n_pair
        margin = survey - across
        f32 = jnp.float32
        block = (width, owned, downward)
        smem = pl.BlockSpec(memory_space=pltpu.SMEM)
        vmem = pl.BlockSpec(memory_space=pltpu.VMEM)
        anywhere = pl.BlockSpec(memory_space=pl.ANY)
        dma = pltpu.SemaphoreType.DMA
        return pl.pallas_call(
            functools.partial(kernel, sizes),
            out_shape=(
                jax.ShapeDtypeStruct(velocity.shape, f32),
                jax.ShapeDtypeStruct(source_now.shape, f32),
                jax.ShapeDtypeStruct(recv_now.shape, f32),
            ),
            in_specs=[smem] * 4 + [vmem] * 3 + [anywhere] * 5,
            out_specs=(anywhere,) * 3,
            scratch_shapes=[
                pltpu.VMEM((2, 2, width + 8, across + 2 * PAD, downward), f32),
                pltpu.VMEM((width, survey, downward), f32),
                pltpu.VMEM((width, across, downward), f32),
                pltpu.VMEM((STEPS, width, across, downward), f32),
                pltpu.VMEM((width, across + 2 * margin, downward), f32),
                pltpu.VMEM((n_shot,) + block, f32),
                pltpu.VMEM((n_shot,) + block, f32),
                pltpu.VMEM((n_shot - 1,) + block, f32),
                pltpu.VMEM((n_shot - 1,) + block, f32),
                pltpu.VMEM(block, f32),
                dma((5,)),
                dma((STEPS, CHUNKS, 2)),
                dma((STEPS, CHUNKS, 2)),
                dma((n_shot,)),
                dma((n_shot,)),
                dma((n_shot,)),
                dma((n_shot,)),
                dma((2, n_shot)),
                dma((n_shot - 1,)),
                dma((n_shot - 1,)),
                dma((3,)),
            ],
            compiler_params=pltpu.CompilerParams(
                collective_id=0, has_side_effects=True, vmem_limit_bytes=48 * 1024 * 1024
            ),
        )(anchors, source_x, source_yz, wavelet, recv_x, recv_yz, record, velocity, source_prev, source_now, recv_prev, recv_now)

    in_specs = (
        P(("region", "tile"), ("shot", "pair"), None),
        P(("region", "shot")),
        P(("region", "shot", "pair"), "tile", None, None),
        P(("region", "shot", "pair"), "tile", None, None),
        P(("region", "shot", "pair"), "tile", None, None),
        P(("region", "shot", "pair"), "tile", None, None),
        P(("region", "shot", "pair")),
        P(("region", "shot", "pair")),
        P(("region", "shot", "pair"), None),
        P(("region", "shot", "pair"), None),
        P(("region", "shot", "pair"), None),
        P(("region", "shot", "pair"), None, None),
    )
    out_specs = (
        P(("region", "tile"), ("shot", "pair"), None),
        P(("region", "shot", "pair"), "tile", None, None),
        P(("region", "shot", "pair"), "tile", None, None),
    )
    return jax.shard_map(shards, mesh=mesh, in_specs=in_specs, out_specs=out_specs, check_vma=False)
```

time: 158 us -> 58.8 us (0.37)
  Pallas kernels: 0 us -> 48.4 us
  waiting for transfers between devices: 46.5 us -> 0 us
  other arithmetic: 42.2 us -> 0 us
  starting transfers between devices: 38.7 us -> 0 us
  between operations: 17 us -> 2.65 us
  blocking collectives: 7.82 us -> 0 us
  local copies, waits for them, and re-layouts: 5.19 us -> 7.42 us
    pallas_call x0 -> x1, Pallas kernels: none -> 48.4 us  [shards(): pl.pallas_call(functools.partial(kernel, sizes), out_shape=(jax.ShapeDtyp...]
    ppermute x12 -> x0, starting transfers between devices: 38.7 us -> none  [the longest x6 30.9 us: padded_2(): lax.ppermute(tail, axis, [(i, (i + 1) % count) for i in range(ends)])]
    reduce_scatter x1 -> x0, waiting for transfers between devices: 24.2 us -> none  [shards(): lax.psum_scatter(placed, ('shot', 'pair'), scatter_dimension=1, tiled=True)]
    ppermute x12 -> x0, waiting for transfers between devices: 22.4 us -> none  [the longest x6 15.9 us: padded_2(): lax.ppermute(head, axis, [((i + 1) % count, i) for i in range(ends)])]
    scatter-add x12 -> x0, other arithmetic: 21.1 us -> none  [deposit(): plane.reshape(-1).at[target].add(amounts, mode='drop').reshape(plane.shape)]
    add x7 -> x0, other arithmetic: 14.8 us -> none  [the longest x6 14.7 us: shards(): updated = 2.0 * interior - older + courant * laplace(extended)]
    all_gather x1 -> x0, blocking collectives: 7.82 us -> none  [shards(): gathered = lax.all_gather(velocity, ('shot', 'pair'), axis=1, tiled=True)]
    concatenate x11 -> x0, other arithmetic: 5.98 us -> none  [padded_2(): jnp.concatenate([lax.ppermute(tail, axis, [(i, (i + 1) % count) for i in...]
  transfers between devices with their start and end apart: 13 -> 0, of which waited for: 11 -> 0; matrix products, arithmetic and copies ran while one was open for 0% -> 0% of each run, Pallas kernels for 0% -> 0%
where the time goes in v1:
time: 58.8 us; the launch traced here: 58.5 us
  Pallas kernels  48.4 us (82%)
  local copies, waits for them, and re-layouts  7.42 us (13%)
  between operations  2.65 us (5%)
    pallas_call x1, Pallas kernels, shards(): pl.pallas_call(functools.partial(kernel, sizes), out_shape=(jax.ShapeDtyp...  48.4 us
    unnamed x22, local copies, waits for them, and re-layouts  7.42 us

profile of v1, /device:TPU:0, one launch (start us, length us, event | category | flops | bytes accessed | tf_op | source)
XLA Modules:
  0.0 58.5 jit_solution(15934791571312532080)
XLA Ops:
  0.6 0.0 copy-start.8
  2.6 0.0 copy-done.8
  2.6 0.0 copy-start.5
  2.6 0.0 copy-start.6
  2.6 0.0 copy-start.7
  2.6 0.6 %copy-done.5 = f32[1,6]{1,0:T(1,128)S(1)} copy-done((f32[1,6]{1,0:T(1,128)S(1)}, f32[1,6]{1,0:T(1,128)}, u32[]{:S(2)}) %copy-start.5) | copy-done | bytes 48
  3.3 0.0 copy-done.6
  3.3 0.0 copy-done.7
  3.3 0.0 copy-start
  3.3 0.9 %copy-done = f32[1,8,64,128]{3,2,1,0:T(8,128)S(1)} copy-done((f32[1,8,64,128]{3,2,1,0:T(8,128)S(1)}, f32[1,8,64,128]{3,2,1,0:T(8,128)}, u32[]{:S(2)}) %copy-start) | copy-done | bytes 262168
  4.2 0.0 copy-start.1
  4.2 0.9 %copy-done.1 = f32[1,8,64,128]{3,2,1,0:T(8,128)S(1)} copy-done((f32[1,8,64,128]{3,2,1,0:T(8,128)S(1)}, f32[1,8,64,128]{3,2,1,0:T(8,128)}, u32[]{:S(2)}) %copy-start.1) | copy-done | bytes 262168
  5.2 0.0 copy-start.2
  5.2 0.9 %copy-done.2 = f32[1,8,64,128]{3,2,1,0:T(8,128)S(1)} copy-done((f32[1,8,64,128]{3,2,1,0:T(8,128)S(1)}, f32[1,8,64,128]{3,2,1,0:T(8,128)}, u32[]{:S(2)}) %copy-start.2) | copy-done | bytes 262168
  6.1 0.0 copy-start.3
  6.1 0.9 %copy-done.3 = f32[1,8,64,128]{3,2,1,0:T(8,128)S(1)} copy-done((f32[1,8,64,128]{3,2,1,0:T(8,128)S(1)}, f32[1,8,64,128]{3,2,1,0:T(8,128)}, u32[]{:S(2)}) %copy-start.3) | copy-done | bytes 262168
  7.1 0.0 copy-start.4
  7.1 0.9 %copy-done.4 = f32[8,32,128]{2,1,0:T(8,128)S(1)} copy-done((f32[8,32,128]{2,1,0:T(8,128)S(1)}, f32[8,32,128]{2,1,0:T(8,128)}, u32[]{:S(2)}) %copy-start.4) | copy-done | bytes 131096
  8.0 48.4 %shard_map.139 = (f32[8,32,128]{2,1,0:T(8,128)S(1)}, f32[1,8,64,128]{3,2,1,0:T(8,128)S(1)}, f32[1,8,64,128]{3,2,1,0:T(8,128)S(1)}) custom-call(s32[1]{0:T(128)S(6)} %copy.19.anchors, s32[1]{0:T(128)S(6)} %copy.20.source_x, s32[1]{0:T(128)S(6)} %copy.21.source_yz, f32[1,6]{1,0:T(1,128)S(1)} %copy-done.5, s32[1,128]{1,0:T(1,128)S(1)} %copy-done.6, ...), custom_call_target="tpu_custom_call" | custom-call | tf_op jit(solution)/shard_map/pallas_call | solution.py:413
  56.4 0.7 %copy.22 = f32[8,32,128]{2,1,0:T(8,128)} copy(f32[8,32,128]{2,1,0:T(8,128)S(1)} %get-tuple-element.6) | data formatting | bytes 262144
  57.1 0.7 %copy.23 = f32[1,8,64,128]{3,2,1,0:T(8,128)} copy(f32[1,8,64,128]{3,2,1,0:T(8,128)S(1)} %get-tuple-element.7) | data formatting | bytes 524288
  57.8 0.7 %copy.24 = f32[1,8,64,128]{3,2,1,0:T(8,128)} copy(f32[1,8,64,128]{3,2,1,0:T(8,128)S(1)} %get-tuple-element.8) | data formatting | bytes 524288
  (1 shorter events, 0.0 us)
Async XLA Ops:
  0.6 2.0 %copy-start.8 = (f32[1,6,128]{2,0,1:T(1,128)S(1)}, f32[1,6,128]{2,0,1:T(1,128)}, u32[]{:S(2)}) copy-start(f32[1,6,128]{2,0,1:T(1,128)} %param.23) | copy-start | bytes 9220
  2.6 0.7 %copy-start.5 = (f32[1,6]{1,0:T(1,128)S(1)}, f32[1,6]{1,0:T(1,128)}, u32[]{:S(2)}) copy-start(f32[1,6]{1,0:T(1,128)} %wavelet.1) | copy-start | bytes 76
  2.6 0.7 %copy-start.6 = (s32[1,128]{1,0:T(1,128)S(1)}, s32[1,128]{1,0:T(1,128)}, u32[]{:S(2)}) copy-start(s32[1,128]{1,0:T(1,128)} %recv_x.1) | copy-start | bytes 1540
  2.6 0.7 %copy-start.7 = (s32[1,128]{1,0:T(1,128)S(1)}, s32[1,128]{1,0:T(1,128)}, u32[]{:S(2)}) copy-start(s32[1,128]{1,0:T(1,128)} %recv_yz.1) | copy-start | bytes 1540
  3.3 0.9 %copy-start = (f32[1,8,64,128]{3,2,1,0:T(8,128)S(1)}, f32[1,8,64,128]{3,2,1,0:T(8,128)}, u32[]{:S(2)}) copy-start(f32[1,8,64,128]{3,2,1,0:T(8,128)} %source_prev.1) | copy-start | bytes 786436
  4.2 0.9 %copy-start.1 = (f32[1,8,64,128]{3,2,1,0:T(8,128)S(1)}, f32[1,8,64,128]{3,2,1,0:T(8,128)}, u32[]{:S(2)}) copy-start(f32[1,8,64,128]{3,2,1,0:T(8,128)} %source_now.1) | copy-start | bytes 786436
  5.2 0.9 %copy-start.2 = (f32[1,8,64,128]{3,2,1,0:T(8,128)S(1)}, f32[1,8,64,128]{3,2,1,0:T(8,128)}, u32[]{:S(2)}) copy-start(f32[1,8,64,128]{3,2,1,0:T(8,128)} %recv_prev.1) | copy-start | bytes 786436
  6.1 0.9 %copy-start.3 = (f32[1,8,64,128]{3,2,1,0:T(8,128)S(1)}, f32[1,8,64,128]{3,2,1,0:T(8,128)}, u32[]{:S(2)}) copy-start(f32[1,8,64,128]{3,2,1,0:T(8,128)} %recv_now.1) | copy-start | bytes 786436
  7.1 0.9 %copy-start.4 = (f32[8,32,128]{2,1,0:T(8,128)S(1)}, f32[8,32,128]{2,1,0:T(8,128)}, u32[]{:S(2)}) copy-start(f32[8,32,128]{2,1,0:T(8,128)} %velocity.1) | copy-start | bytes 393220

commit v2 on v1

--- a/solution.py
+++ b/solution.py
@@ -395,6 +395,16 @@
     last.wait()
 
 
+def deliver(*refs):
+    sem = refs[-1]
+    count = (len(refs) - 1) // 2
+    copies = [pltpu.make_async_copy(refs[i], refs[count + i], sem.at[i]) for i in range(count)]
+    for copy in copies:
+        copy.start()
+    for copy in copies:
+        copy.wait()
+
+
 def solution(mesh):
     sizes = (mesh.shape["tile"], mesh.shape["shot"], mesh.shape["pair"])
     n_shot, n_pair = sizes[1:]
@@ -410,7 +420,7 @@
         vmem = pl.BlockSpec(memory_space=pltpu.VMEM)
         anywhere = pl.BlockSpec(memory_space=pl.ANY)
         dma = pltpu.SemaphoreType.DMA
-        return pl.pallas_call(
+        results = pl.pallas_call(
             functools.partial(kernel, sizes),
             out_shape=(
                 jax.ShapeDtypeStruct(velocity.shape, f32),
@@ -418,7 +428,7 @@
                 jax.ShapeDtypeStruct(recv_now.shape, f32),
             ),
             in_specs=[smem] * 4 + [vmem] * 3 + [anywhere] * 5,
-            out_specs=(anywhere,) * 3,
+            out_specs=(vmem,)*3,
             scratch_shapes=[
                 pltpu.VMEM((2, 2, width + 8, across + 2 * PAD, downward), f32),
                 pltpu.VMEM((width, survey, downward), f32),
@@ -443,9 +453,17 @@
                 dma((3,)),
             ],
             compiler_params=pltpu.CompilerParams(
-                collective_id=0, has_side_effects=True, vmem_limit_bytes=48 * 1024 * 1024
+                collective_id=0, has_side_effects=True, vmem_limit_bytes=63 * 1024 * 1024
             ),
         )(anchors, source_x, source_yz, wavelet, recv_x, recv_yz, record, velocity, source_prev, source_now, recv_prev, recv_now)
+
+        return pl.pallas_call(
+            deliver,
+            out_shape=[jax.ShapeDtypeStruct(result.shape, f32) for result in results],
+            in_specs=[vmem]*3,
+            out_specs=[anywhere] * 3,
+            scratch_shapes=[dma((3,))],
+        )(*results)
 
     in_specs = (
         P(("region", "tile"), ("shot", "pair"), None),

time: 58.8 us -> 55.1 us (0.937)
  local copies, waits for them, and re-layouts: 7.42 us -> 0.6 us
  Pallas kernels: 48.4 us -> 51.7 us
    unnamed x22 -> x3, local copies, waits for them, and re-layouts: 7.42 us -> 0.6 us
    pallas_call x0 -> x1, Pallas kernels: none -> 1.95 us  [shards(): pl.pallas_call(deliver, out_shape=[jax.ShapeDtypeStruct(result.shape, f32...]
    pallas_call x1, Pallas kernels: 48.4 us -> 49.7 us  [shards(): pl.pallas_call(functools.partial(kernel, sizes), out_shape=(jax.ShapeDtyp...]
where the time goes in v2:
time: 55.1 us; the launch traced here: 54.9 us
  Pallas kernels  51.7 us (94%)
  between operations  2.61 us (5%)
  local copies, waits for them, and re-layouts  0.6 us (1%)
    pallas_call x1, Pallas kernels, shards(): pl.pallas_call(functools.partial(kernel, sizes), out_shape=(jax.ShapeDtyp...  49.7 us
    pallas_call x1, Pallas kernels, shards(): pl.pallas_call(deliver, out_shape=[jax.ShapeDtypeStruct(result.shape, f32...  1.95 us

profile of v2, /device:TPU:0, one launch (start us, length us, event | category | flops | bytes accessed | tf_op | source)
XLA Modules:
  0.0 54.9 jit_solution(10342253289554203199)
XLA Ops:
  0.6 0.0 copy-start
  2.6 0.0 copy-done
  2.6 0.6 %copy.15.record = f32[1,6,128]{2,1,0:T(8,128)} copy(f32[1,6,128]{2,0,1:T(1,128)S(1)} %copy-done) | data formatting | bytes 6144 | tf_op args[11]
  3.2 49.7 %shard_map.139 = (f32[8,32,128]{2,1,0:T(8,128)}, f32[1,8,64,128]{3,2,1,0:T(8,128)}, f32[1,8,64,128]{3,2,1,0:T(8,128)}) custom-call(s32[1]{0:T(128)S(6)} %copy.16.anchors, s32[1]{0:T(128)S(6)} %copy.17.source_x, s32[1]{0:T(128)S(6)} %copy.18.source_yz, f32[1,6]{1,0:T(1,128)} %wavelet.1, s32[1,128]{1,0:T(1,128)} %recv_x.1, s32[1,128]{1,0:T(1,128)} %recv_yz.1, ...), custom_call_target="tpu_custom_call" | custom-call | tf_op jit(solution)/shard_map/pallas_call | solution.py:423
  52.9 2.0 %shard_map.140 = (f32[8,32,128]{2,1,0:T(8,128)}, f32[1,8,64,128]{3,2,1,0:T(8,128)}, f32[1,8,64,128]{3,2,1,0:T(8,128)}) custom-call(f32[8,32,128]{2,1,0:T(8,128)} %get-tuple-element.6.refs_0_, f32[1,8,64,128]{3,2,1,0:T(8,128)} %get-tuple-element.7.refs_1_, f32[1,8,64,128]{3,2,1,0:T(8,128)} %get-tuple-element.8.refs_2_), custom_call_target="tpu_custom_call" | custom-call | tf_op jit(solution)/shard_map/pallas_call | solution.py:460
Async XLA Ops:
  0.6 2.0 %copy-start = (f32[1,6,128]{2,0,1:T(1,128)S(1)}, f32[1,6,128]{2,0,1:T(1,128)}, u32[]{:S(2)}) copy-start(f32[1,6,128]{2,0,1:T(1,128)} %param.23) | copy-start | bytes 9220

commit v3 on v2

--- a/solution.py
+++ b/solution.py
@@ -14,7 +14,7 @@
 courant_scale = 0.1
 
 PAD = 8
-CHUNKS = 4
+CHUNKS = 2
 
 
 def kernel(
@@ -38,12 +38,12 @@
     speed,
     courant,
     injected,
+    pending,
     stacked,
     mate_out,
     mate_in,
     shot_out,
     shot_in,
-    total,
     load_sem,
     halo_send,
     halo_recv,
@@ -196,8 +196,8 @@
     pick = jnp.where(cell == place, 1.0, 0.0).astype(jnp.bfloat16)
     at_depth = lax.broadcasted_iota(jnp.int32, (downward, receivers), 0) == depth
 
-    def inject(n, _):
-        amount = record[0, pl.ds(n, 1), :]
+    def inject(n):
+        amount = record[n]
         high = amount.astype(jnp.bfloat16).astype(jnp.float32)
         rest = amount - high
         middle = rest.astype(jnp.bfloat16).astype(jnp.float32)
@@ -208,10 +208,92 @@
             dense = dense + lax.dot_general(
                 pick, spread, (((1,), (1,)), ((), ())), preferred_element_type=jnp.float32
             )
-        injected[n] = dense.reshape(width, across, downward)
+        injected[...] = dense.reshape(width, across, downward)
+
+    lane = lax.broadcasted_iota(jnp.int32, (1, 1, downward), 2)
+    behind = [jnp.where(lane >= r, stencil_weights[r], 0.0) for r in range(1, 5)]
+    ahead = [jnp.where(lane < downward - r, stencil_weights[r], 0.0) for r in range(1, 5)]
+    shape = (width, 8, downward)
+    local_cell = (
+        lax.broadcasted_iota(jnp.int32, shape, 0) * (across * downward)
+        + lax.broadcasted_iota(jnp.int32, shape, 1) * downward
+        + lax.broadcasted_iota(jnp.int32, shape, 2)
+    )
+    source_cell = (source_x[0] - first) * (across * downward) + source_yz[0]
+
+    def prepare(s, slot, y0):
+        at = pl.multiple_of(PAD + y0, 8)
+        for f in range(2):
+            centre = field[slot, f, 4 : 4 + width, pl.ds(at, 8), :]
+            sums = (3.0 * stencil_weights[0]) * centre
+            for r in range(1, 5):
+                layers = []
+                for j in range(width):
+                    layer = [centre[i : i + 1] for i in (j - r, j + r) if 0 <= i < width]
+                    layers.append(layer[0] if len(layer) == 1 else layer[0] + layer[1])
+                near = jnp.concatenate(layers, axis=0)
+                near = near + field[slot, f, 4 : 4 + width, pl.ds(at - r, 8), :]
+                near = near + field[slot, f, 4 : 4 + width, pl.ds(at + r, 8), :]
+                sums = sums + stencil_weights[r] * near
+                sums = sums + behind[r - 1] * pltpu.roll(centre, r, 2)
+                sums = sums + ahead[r - 1] * pltpu.roll(centre, downward - r, 2)
+            older = field[1 - slot, f, 4 : 4 + width, pl.ds(at, 8), :]
+            pending[f, :, pl.ds(y0, 8), :] = sums
+            fresh = 2.0 * centre - older
+            if f == 0:
+                fresh = fresh + jnp.where(local_cell == source_cell - y0 * downward, wavelet[0, s], 0.0)
+            else:
+                fresh = fresh + injected[:, pl.ds(y0, 8), :]
+            field[1 - slot, f, 4 : 4 + width, pl.ds(at, 8), :] = fresh
+
+    def complete(slot, y0):
+        at = pl.multiple_of(PAD + y0, 8)
+        gain = courant[:, pl.ds(y0, 8), :]
+        results = []
+        for f in range(2):
+            low = field[slot, f, 0:4, pl.ds(at, 8), :]
+            high = field[slot, f, 4 + width : 8 + width, pl.ds(at, 8), :]
+            below, above = [], []
+            for j in range(4):
+                term = stencil_weights[j + 1] * low[3:4]
+                for r in range(j + 2, 5):
+                    term = term + stencil_weights[r] * low[4 + j - r : 5 + j - r]
+                below.append(term)
+                term = stencil_weights[4 - j] * high[0:1]
+                for r in range(5 - j, 5):
+                    term = term + stencil_weights[r] * high[j - 4 + r : j - 3 + r]
+                above.append(term)
+            middle = [jnp.zeros((width - 8, 8, downward), jnp.float32)] if width > 8 else []
+            outer = jnp.concatenate(below + middle + above, axis=0)
+            fresh = field[1 - slot, f, 4 : 4 + width, pl.ds(at, 8), :] + gain * (pending[f, :, pl.ds(y0, 8), :] + outer)
+            field[1 - slot, f, 4 : 4 + width, pl.ds(at, 8), :] = fresh
+            results.append(fresh)
+        spot = pl.ds(pl.multiple_of(margin + y0, 8), 8)
+        stacked[:, spot, :] = stacked[:, spot, :] + results[0] * results[1]
+
+    def settle(s, c, _):
+        @pl.when(has_low)
+        def _():
+            halo(s, lax.rem(s, 2), c, 0).wait_send()
+
+        @pl.when(has_high)
+        def _():
+            halo(s, lax.rem(s, 2), c, 1).wait_send()
+
         return 0
 
-    lax.fori_loop(0, STEPS, inject, 0)
+    def prepare_all(s):
+        inject(s)
+
+        def ready(t, _):
+            prepare(s, lax.rem(s, 2), pl.multiple_of(t * 8, 8))
+            return 0
+
+        lax.fori_loop(0, across // 8, ready, 0)
+
+    for copy in loads[:4]:
+        copy.wait()
+    prepare_all(0)
 
     for k in range(1, n_shot):
         origin = lax.rem(shot + n_shot - k, n_shot)
@@ -222,8 +304,7 @@
         pltpu.make_async_remote_copy(
             block, block, mate_speed_send.at[k], mate_speed_recv.at[k], device_id={"pair": mate}, device_id_type=MESH
         ).start()
-    for copy in loads:
-        copy.wait()
+    loads[4].wait()
     for k in range(n_shot):
         origin = lax.rem(shot + n_shot - k, n_shot)
         pltpu.make_async_remote_copy(
@@ -244,43 +325,6 @@
 
     lax.fori_loop(0, width, refresh, 0)
 
-    lane = lax.broadcasted_iota(jnp.int32, (1, 1, downward), 2)
-    behind = [jnp.where(lane >= r, stencil_weights[r], 0.0) for r in range(1, 5)]
-    ahead = [jnp.where(lane < downward - r, stencil_weights[r], 0.0) for r in range(1, 5)]
-    shape = (width, 8, downward)
-    local_cell = (
-        lax.broadcasted_iota(jnp.int32, shape, 0) * (across * downward)
-        + lax.broadcasted_iota(jnp.int32, shape, 1) * downward
-        + lax.broadcasted_iota(jnp.int32, shape, 2)
-    )
-    source_cell = (source_x[0] - first) * (across * downward) + source_yz[0]
-
-    def update(s, slot, y0):
-        at = pl.multiple_of(PAD + y0, 8)
-        gain = courant[:, pl.ds(y0, 8), :]
-        results = []
-        for f in range(2):
-            column = field[slot, f, :, pl.ds(at, 8), :]
-            centre = column[4 : 4 + width]
-            sums = (3.0 * stencil_weights[0]) * centre
-            for r in range(1, 5):
-                near = column[4 - r : 4 - r + width] + column[4 + r : 4 + r + width]
-                near = near + field[slot, f, 4 : 4 + width, pl.ds(at - r, 8), :]
-                near = near + field[slot, f, 4 : 4 + width, pl.ds(at + r, 8), :]
-                sums = sums + stencil_weights[r] * near
-                sums = sums + behind[r - 1] * pltpu.roll(centre, r, 2)
-                sums = sums + ahead[r - 1] * pltpu.roll(centre, downward - r, 2)
-            older = field[1 - slot, f, 4 : 4 + width, pl.ds(at, 8), :]
-            fresh = 2.0 * centre - older + gain * sums
-            if f == 0:
-                fresh = fresh + jnp.where(local_cell == source_cell - y0 * downward, wavelet[0, s], 0.0)
-            else:
-                fresh = fresh + injected[s, :, pl.ds(y0, 8), :]
-            field[1 - slot, f, 4 : 4 + width, pl.ds(at, 8), :] = fresh
-            results.append(fresh)
-        spot = pl.ds(pl.multiple_of(margin + y0, 8), 8)
-        stacked[:, spot, :] = stacked[:, spot, :] + results[0] * results[1]
-
     def step(s, _):
         slot = lax.rem(s, 2)
 
@@ -293,16 +337,8 @@
             def _():
                 halo(s, slot, c, 0).wait_recv()
 
-            @pl.when(jnp.logical_and(has_low, s > 0))
-            def _():
-                halo(s - 1, 1 - slot, c, 0).wait_send()
-
-            @pl.when(jnp.logical_and(has_high, s > 0))
-            def _():
-                halo(s - 1, 1 - slot, c, 1).wait_send()
-
             def tiles(t, _):
-                update(s, slot, pl.multiple_of(c * rows + t * 8, 8))
+                complete(slot, pl.multiple_of(c * rows + t * 8, 8))
                 return 0
 
             lax.fori_loop(0, rows // 8, tiles, 0)
@@ -318,6 +354,12 @@
             return 0
 
         lax.fori_loop(0, CHUNKS, chunk, 0)
+
+        @pl.when(s < STEPS - 1)
+        def _():
+            lax.fori_loop(0, CHUNKS, functools.partial(settle, s), 0)
+            prepare_all(s + 1)
+
         return 0
 
     lax.fori_loop(0, STEPS, step, 0)
@@ -373,9 +415,7 @@
     for k in range(1, n_shot):
         shot_copy(k).wait_recv()
         mine = mine + shot_in[k - 1]
-    total[...] = mine
-    last = pltpu.make_async_copy(total, image_out, out_sem.at[2])
-    last.start()
+    image_out[...] = mine
 
     for c in range(CHUNKS):
         @pl.when(has_low)
@@ -392,7 +432,6 @@
         shot_copy(k).wait_send()
     for copy in stores:
         copy.wait()
-    last.wait()
 
 
 def deliver(*refs):
@@ -433,13 +472,13 @@
                 pltpu.VMEM((2, 2, width + 8, across + 2 * PAD, downward), f32),
                 pltpu.VMEM((width, survey, downward), f32),
                 pltpu.VMEM((width, across, downward), f32),
-                pltpu.VMEM((STEPS, width, across, downward), f32),
+                pltpu.VMEM((width, across, downward), f32),
+                pltpu.VMEM((2, width, across, downward), f32),
                 pltpu.VMEM((width, across + 2 * margin, downward), f32),
                 pltpu.VMEM((n_shot,) + block, f32),
                 pltpu.VMEM((n_shot,) + block, f32),
                 pltpu.VMEM((n_shot - 1,) + block, f32),
                 pltpu.VMEM((n_shot - 1,) + block, f32),
-                pltpu.VMEM(block, f32),
                 dma((5,)),
                 dma((STEPS, CHUNKS, 2)),
                 dma((STEPS, CHUNKS, 2)),
@@ -450,12 +489,12 @@
                 dma((2, n_shot)),
                 dma((n_shot - 1,)),
                 dma((n_shot - 1,)),
-                dma((3,)),
+                dma((2,)),
             ],
             compiler_params=pltpu.CompilerParams(
                 collective_id=0, has_side_effects=True, vmem_limit_bytes=63 * 1024 * 1024
             ),
-        )(anchors, source_x, source_yz, wavelet, recv_x, recv_yz, record, velocity, source_prev, source_now, recv_prev, recv_now)
+        )(anchors, source_x, source_yz, wavelet, recv_x, recv_yz, jnp.swapaxes(record, 0, 1), velocity, source_prev, source_now, recv_prev, recv_now)
 
         return pl.pallas_call(
             deliver,

time: 55.1 us -> 51.8 us (0.940)
  Pallas kernels: 51.7 us -> 49 us
  local copies, waits for them, and re-layouts: 0.6 us -> 0 us
    pallas_call x1, Pallas kernels: 49.7 us -> 47 us  [shards(): pl.pallas_call(functools.partial(kernel, sizes), out_shape=(jax.ShapeDtyp...]
    unnamed x3 -> x0, local copies, waits for them, and re-layouts: 0.6 us -> none
where the time goes in v3:
time: 51.8 us; the launch traced here: 51.6 us
  Pallas kernels  49 us (95%)
  between operations  2.58 us (5%)
    pallas_call x1, Pallas kernels, shards(): pl.pallas_call(functools.partial(kernel, sizes), out_shape=(jax.ShapeDtyp...  47 us
    pallas_call x1, Pallas kernels, shards(): pl.pallas_call(deliver, out_shape=[jax.ShapeDtypeStruct(result.shape, f32...  1.95 us

profile of v3, /device:TPU:0, one launch (start us, length us, event | category | flops | bytes accessed | tf_op | source)
XLA Modules:
  0.0 51.6 jit_solution(4390866757407641277)
XLA Ops:
  2.6 47.0 %shard_map.139 = (f32[8,32,128]{2,1,0:T(8,128)}, f32[1,8,64,128]{3,2,1,0:T(8,128)}, f32[1,8,64,128]{3,2,1,0:T(8,128)}) custom-call(s32[1]{0:T(128)S(6)} %copy.15.anchors, s32[1]{0:T(128)S(6)} %copy.16.source_x, s32[1]{0:T(128)S(6)} %copy.17.source_yz, f32[1,6]{1,0:T(1,128)} %wavelet.1, s32[1,128]{1,0:T(1,128)} %recv_x.1, s32[1,128]{1,0:T(1,128)} %recv_yz.1, ...), custom_call_target="tpu_custom_call" | custom-call | tf_op jit(solution)/shard_map/pallas_call | solution.py:462
  49.6 2.0 %shard_map.140 = (f32[8,32,128]{2,1,0:T(8,128)}, f32[1,8,64,128]{3,2,1,0:T(8,128)}, f32[1,8,64,128]{3,2,1,0:T(8,128)}) custom-call(f32[8,32,128]{2,1,0:T(8,128)} %get-tuple-element.6.refs_0_, f32[1,8,64,128]{3,2,1,0:T(8,128)} %get-tuple-element.7.refs_1_, f32[1,8,64,128]{3,2,1,0:T(8,128)} %get-tuple-element.8.refs_2_), custom_call_target="tpu_custom_call" | custom-call | tf_op jit(solution)/shard_map/pallas_call | solution.py:499

commit v4 on v3

--- a/solution.py
+++ b/solution.py
@@ -15,6 +15,7 @@
 
 PAD = 8
 CHUNKS = 2
+PIECES = 2
 
 
 def kernel(
@@ -372,50 +373,47 @@
     for copy in stores:
         copy.start()
 
-    def contribution(s, p):
-        return stacked[:, pl.ds((s * n_pair + p) * owned + margin - start_row, owned), :]
-
-    for k in range(n_shot):
-        mate_out[k] = contribution(lax.rem(shot + k, n_shot), mate)
-        pltpu.make_async_remote_copy(
-            mate_out.at[k],
-            mate_in.at[k],
-            mate_sem.at[0, k],
-            mate_sem.at[1, k],
-            device_id={"pair": mate},
-            device_id_type=MESH,
-        ).start()
-
-    def mate_copy(k):
+    depth_of = width // PIECES
+    pieces = [pl.ds(i * depth_of, depth_of) for i in range(PIECES)]
+
+    def contribution(s, p, layers):
+        return stacked[layers, pl.ds((s * n_pair + p) * owned + margin - start_row, owned), :]
+
+    def mate_copy(k, i):
         return pltpu.make_async_remote_copy(
-            mate_out.at[k],
-            mate_in.at[k],
-            mate_sem.at[0, k],
-            mate_sem.at[1, k],
+            mate_out.at[k, pieces[i]],
+            mate_in.at[k, pieces[i]],
+            mate_sem.at[0, k, i],
+            mate_sem.at[1, k, i],
             device_id={"pair": mate},
             device_id_type=MESH,
         )
 
-    def shot_copy(k):
+    def shot_copy(k, i):
         return pltpu.make_async_remote_copy(
-            shot_out.at[k - 1],
-            shot_in.at[k - 1],
-            shot_send.at[k - 1],
-            shot_recv.at[k - 1],
+            shot_out.at[k - 1, pieces[i]],
+            shot_in.at[k - 1, pieces[i]],
+            shot_send.at[k - 1, i],
+            shot_recv.at[k - 1, i],
             device_id={"shot": lax.rem(shot + k, n_shot)},
             device_id_type=MESH,
         )
 
-    for k in range(1, n_shot):
-        mate_copy(k).wait_recv()
-        shot_out[k - 1] = contribution(lax.rem(shot + k, n_shot), pair) + mate_in[k]
-        shot_copy(k).start()
-    mate_copy(0).wait_recv()
-    mine = contribution(shot, pair) + mate_in[0]
-    for k in range(1, n_shot):
-        shot_copy(k).wait_recv()
-        mine = mine + shot_in[k - 1]
-    image_out[...] = mine
+    order = [(k, i) for k in list(range(1, n_shot)) + [0] for i in range(PIECES)]
+    travelling = order[: (n_shot - 1) * PIECES]
+    for k, i in order:
+        mate_out[k, pieces[i]] = contribution(lax.rem(shot + k, n_shot), mate, pieces[i])
+        mate_copy(k, i).start()
+    for k, i in travelling:
+        mate_copy(k, i).wait_recv()
+        shot_out[k - 1, pieces[i]] = contribution(lax.rem(shot + k, n_shot), pair, pieces[i]) + mate_in[k, pieces[i]]
+        shot_copy(k, i).start()
+    for i in range(PIECES):
+        mate_copy(0, i).wait_recv()
+        image_out[pieces[i]] = contribution(shot, pair, pieces[i]) + mate_in[0, pieces[i]]
+    for k, i in travelling:
+        shot_copy(k, i).wait_recv()
+        image_out[pieces[i]] = image_out[pieces[i]] + shot_in[k - 1, pieces[i]]
 
     for c in range(CHUNKS):
         @pl.when(has_low)
@@ -426,10 +424,10 @@
         def _():
             halo(STEPS - 1, (STEPS - 1) % 2, c, 1).wait_send()
 
-    for k in range(n_shot):
-        mate_copy(k).wait_send()
-    for k in range(1, n_shot):
-        shot_copy(k).wait_send()
+    for k, i in order:
+        mate_copy(k, i).wait_send()
+    for k, i in travelling:
+        shot_copy(k, i).wait_send()
     for copy in stores:
         copy.wait()
 
@@ -467,7 +465,7 @@
                 jax.ShapeDtypeStruct(recv_now.shape, f32),
             ),
             in_specs=[smem] * 4 + [vmem] * 3 + [anywhere] * 5,
-            out_specs=(vmem,)*3,
+            out_specs=(vmem, anywhere, anywhere),
             scratch_shapes=[
                 pltpu.VMEM((2, 2, width + 8, across + 2 * PAD, downward), f32),
                 pltpu.VMEM((width, survey, downward), f32),
@@ -486,9 +484,9 @@
                 dma((n_shot,)),
                 dma((n_shot,)),
                 dma((n_shot,)),
-                dma((2, n_shot)),
-                dma((n_shot - 1,)),
-                dma((n_shot - 1,)),
+                dma((2, n_shot, PIECES)),
+                dma((n_shot - 1, PIECES)),
+                dma((n_shot - 1, PIECES)),
                 dma((2,)),
             ],
             compiler_params=pltpu.CompilerParams(

time: 51.8 us -> 51.5 us (level)
  no operation moved by 1% of the time
where the time goes in v4:
time: 51.5 us; the launch traced here: 51.3 us
  Pallas kernels  48.7 us (95%)
  between operations  2.58 us (5%)
    pallas_call x1, Pallas kernels, shards(): pl.pallas_call(functools.partial(kernel, sizes), out_shape=(jax.ShapeDtyp...  46.8 us
    pallas_call x1, Pallas kernels, shards(): pl.pallas_call(deliver, out_shape=[jax.ShapeDtypeStruct(result.shape, f32...  1.95 us

profile of v4, /device:TPU:0, one launch (start us, length us, event | category | flops | bytes accessed | tf_op | source)
XLA Modules:
  0.0 51.3 jit_solution(405201987095821077)
XLA Ops:
  2.6 46.8 %shard_map.139 = (f32[8,32,128]{2,1,0:T(8,128)}, f32[1,8,64,128]{3,2,1,0:T(8,128)}, f32[1,8,64,128]{3,2,1,0:T(8,128)}) custom-call(s32[1]{0:T(128)S(6)} %copy.15.anchors, s32[1]{0:T(128)S(6)} %copy.16.source_x, s32[1]{0:T(128)S(6)} %copy.17.source_yz, f32[1,6]{1,0:T(1,128)} %wavelet.1, s32[1,128]{1,0:T(1,128)} %recv_x.1, s32[1,128]{1,0:T(1,128)} %recv_yz.1, ...), custom_call_target="tpu_custom_call" | custom-call | tf_op jit(solution)/shard_map/pallas_call | solution.py:460
  49.4 2.0 %shard_map.140 = (f32[8,32,128]{2,1,0:T(8,128)}, f32[1,8,64,128]{3,2,1,0:T(8,128)}, f32[1,8,64,128]{3,2,1,0:T(8,128)}) custom-call(f32[8,32,128]{2,1,0:T(8,128)} %get-tuple-element.6.refs_0_, f32[1,8,64,128]{3,2,1,0:T(8,128)} %get-tuple-element.7.refs_1_, f32[1,8,64,128]{3,2,1,0:T(8,128)} %get-tuple-element.8.refs_2_), custom_call_target="tpu_custom_call" | custom-call | tf_op jit(solution)/shard_map/pallas_call | solution.py:497
